TPU v7x, 32 devices: a whole 2x2x4 slice. The times are simulated.
32 devices in a mesh: brick: 16 (over z, y, x), seed: 2 (over core).
Axes of the slice: x: 2, y: 2, z: 4, core: 2. Of those that a mesh axis runs over, the one named last changes fastest.
Arguments:
- seed_data: float32 [4, 65536], P(None, ('brick', 'seed')), as said below
- block_slot: int32 [512], replicated, may hold values from 0 to 511, as said below
- candidates: int32 [256, 8], P('brick', 'seed'), may hold values from 0 to 511, as said below
- cand_count: int32 [256], P('brick'), may hold values from 1 to 8
- pixel_mass: float32 [256, 512], P('brick'), may hold values from 0.1 to 1
Outputs:
- seed_stats: float32 [4, 65536], P(None, ('brick', 'seed'))
Inputs may be any that keep to these rules, and one draw needn't show every extreme that they name: A permutation of the storage positions. Block g is homed in brick g // 32 and stored on the device of brick index block_slot[g] // 32 and seed index (block_slot[g] // 16) % 2. For each brick and seed index, exactly 16 blocks homed in that brick are stored at that seed index; one device stores at most 1 block homed in any one brick, and some devices reach it. `candidates`: row t holds 8 distinct ids of blocks homed in tile t's brick, between (t // 16) * 32 and that plus 32 - 1. `seed_data`: the seeds of a block lie in the region of its home brick: second coordinate between h * 2 and (h + 1) * 2 for home brick h, first between 0 and 1, third between 0 and 8.
All inputs are finite; a program needn't handle non-finite values.
Results may differ from a plain program's by a relative error of at most 0.0003.
Values sent between devices are 32-bit elements; how exact they have to be, the bound alone decides.
No kernel may reach another device: no remote copies, remote signals or barrier semaphores. Data moves between devices by JAX's collectives and lax.ppermute only.
A program may use at most 64 MiB of HBM per device.

v0:
```python
import math
import jax
import jax.numpy as jnp
from jax import lax
from jax.sharding import PartitionSpec as P

TILES_Y = 2
TILES_Z = 8
blur_eps = 0.5
far_score = -1e30


def joined(value, axis, join):
    pieces = jax.tree.map(lambda part: lax.all_gather(part, axis), value)
    head = jax.tree.map(lambda part: part[0], pieces)
    tail = jax.tree.map(lambda part: part[1:], pieces)
    running, _ = lax.scan(lambda running, share: (join(running, share), None), head, tail)
    return running


def pixel_points(brick_ids, tile_ids):
    within = jnp.arange(512, dtype=jnp.int32)
    tile_x = tile_ids // (TILES_Y * TILES_Z)
    tile_y = tile_ids // TILES_Z % TILES_Y
    tile_z = tile_ids % TILES_Z
    offset_x = ((within // 64).astype(jnp.float32) + 0.5) / 8.0
    offset_y = ((within // 8 % 8).astype(jnp.float32) + 0.5) / 8.0
    offset_z = ((within % 8).astype(jnp.float32) + 0.5) / 8.0
    point_x = tile_x.astype(jnp.float32)[:, None] + offset_x[None, :]
    point_y = (brick_ids * TILES_Y + tile_y).astype(jnp.float32)[:, None] + offset_y[None, :]
    point_z = tile_z.astype(jnp.float32)[:, None] + offset_z[None, :]
    return jnp.stack([point_x, point_y, point_z])


def tile_scores(points, seed_cols, valid_cols):
    differ = points[0][:, :, None] - seed_cols[0][:, None, :]
    distance = differ * differ
    differ = points[1][:, :, None] - seed_cols[1][:, None, :]
    distance = distance + differ * differ
    differ = points[2][:, :, None] - seed_cols[2][:, None, :]
    distance = distance + differ * differ
    scores = (seed_cols[3][:, None, :] - distance) / blur_eps
    return jnp.where(valid_cols[:, None, :], scores, far_score)


def combine_stats(left_pair, right_pair):
    left_peak, left_total = left_pair
    right_peak, right_total = right_pair
    joint_peak = jnp.maximum(left_peak, right_peak)
    joint_total = left_total * jnp.exp(left_peak - joint_peak) + right_total * jnp.exp(
        right_peak - joint_peak
    )
    return (joint_peak, joint_total)


def body(seed_data, block_slot, candidates, cand_count, pixel_mass):
    brick_index = lax.axis_index("brick")
    shard_index = lax.axis_index("seed")
    brick_size = lax.axis_size("brick")
    seed_size = lax.axis_size("seed")
    lane_count = seed_data.shape[1] // 128
    home_blocks = lane_count * seed_size
    total_blocks = block_slot.shape[0]
    capacity = max(1, lane_count // brick_size)
    tile_count, slot_count = candidates.shape
    positions = jnp.arange(total_blocks, dtype=jnp.int32)
    inverse = jnp.zeros((total_blocks,), jnp.int32).at[block_slot].set(positions)
    home_of_pos = inverse // home_blocks
    grouped = home_of_pos.reshape(brick_size * seed_size, lane_count)
    lane_ids = jnp.arange(lane_count, dtype=jnp.int32)
    before = lane_ids[:, None] < lane_ids[None, :]
    same_home = grouped[:, :, None] == grouped[:, None, :]
    rank_of_pos = jnp.sum(same_home & before[None], axis=1).reshape(total_blocks)
    own_first = (brick_index * seed_size + shard_index) * lane_count
    own_home = lax.dynamic_slice_in_dim(home_of_pos, own_first, lane_count)
    own_rank = lax.dynamic_slice_in_dim(rank_of_pos, own_first, lane_count)
    own_seeds = seed_data.reshape(4, lane_count, 128)
    outgoing = jnp.zeros((4, brick_size * capacity, 128), jnp.float32)
    outgoing = outgoing.at[:, own_home * capacity + own_rank, :].set(own_seeds)
    incoming = lax.all_to_all(outgoing, "brick", split_axis=1, concat_axis=1, tiled=True)
    home_slots = lax.dynamic_slice_in_dim(block_slot, brick_index * home_blocks, home_blocks)
    home_shard = home_slots // lane_count % seed_size
    home_owner = home_slots // home_blocks
    home_rank = rank_of_pos[home_slots]
    home_flat = home_owner * capacity + home_rank
    members = jnp.arange(home_blocks, dtype=jnp.int32)
    earlier = members[:, None] < members[None, :]
    queue_pos = jnp.sum((home_shard[:, None] == home_shard[None, :]) & earlier, axis=0)
    panel_index = home_shard * lane_count + queue_pos
    is_mine = home_shard == shard_index
    target = jnp.where(is_mine, queue_pos, lane_count)
    compact = jnp.zeros((4, lane_count, 128), jnp.float32)
    compact = compact.at[:, target, :].set(incoming[:, home_flat, :], mode="drop")
    seed_panel = lax.all_gather(compact, "seed", axis=1, tiled=True)
    start_totals = jnp.zeros((4, home_blocks, 128), jnp.float32)
    group_size = math.gcd(tile_count, 8)
    step_count = tile_count // group_size
    slot_cols = slot_count * 128
    slot_ids = shard_index * slot_count + jnp.arange(slot_count, dtype=jnp.int32)
    cand_panel = panel_index[candidates - brick_index * home_blocks]
    valid_all = jnp.repeat(slot_ids[None, :] < cand_count[:, None], 128, axis=1)
    brick_ids = jnp.zeros((group_size,), jnp.int32) + brick_index

    def group_scores(step_index):
        first_tile = step_index * group_size
        tile_ids = first_tile + jnp.arange(group_size, dtype=jnp.int32)
        points = pixel_points(brick_ids, tile_ids)
        chosen = lax.dynamic_slice_in_dim(cand_panel, first_tile, group_size)
        seed_cols = seed_panel[:, chosen.reshape(-1), :].reshape(4, group_size, slot_cols)
        valid_cols = lax.dynamic_slice_in_dim(valid_all, first_tile, group_size)
        return (tile_scores(points, seed_cols, valid_cols), points, chosen, valid_cols)

    def local_both(step_index):
        scores, points, chosen, valid_cols = group_scores(step_index)
        pixel_peak = jnp.max(scores, axis=2)
        raw_share = jnp.where(valid_cols[:, None, :], jnp.exp(scores - pixel_peak[:, :, None]), 0.0)
        return (pixel_peak, jnp.sum(raw_share, axis=2))

    step_ids = jnp.arange(step_count, dtype=jnp.int32)
    peak_local, total_local = lax.map(local_both, step_ids)
    pixel_peak, pixel_total = joined((peak_local, total_local), "seed", combine_stats)

    def contribute(totals, step_bits):
        step_index, group_peak, group_total = step_bits
        scores, points, chosen, valid_cols = group_scores(step_index)
        raw_share = jnp.where(valid_cols[:, None, :], jnp.exp(scores - group_peak[:, :, None]), 0.0)
        shares = raw_share / group_total[:, :, None]
        pixel_weight = lax.dynamic_slice_in_dim(pixel_mass, step_index * group_size, group_size)
        features = jnp.stack(
            [
                pixel_weight,
                pixel_weight * points[0],
                pixel_weight * points[1],
                pixel_weight * points[2],
            ]
        )
        moments = jnp.einsum("fgi,gic->fgc", features, shares, precision=lax.Precision.HIGHEST)
        totals = totals.at[:, chosen.reshape(-1), :].add(
            moments.reshape(4, group_size * slot_count, 128)
        )
        return (totals, None)

    totals, unused = lax.scan(contribute, start_totals, (step_ids, pixel_peak, pixel_total))
    raw_target = home_owner * (seed_size * capacity) + home_shard * capacity + home_rank
    outgoing_raw = jnp.zeros((4, brick_size * seed_size * capacity, 128), jnp.float32)
    outgoing_raw = outgoing_raw.at[:, raw_target, :].set(totals[:, panel_index, :])
    arrived = lax.all_to_all(outgoing_raw, "brick", split_axis=1, concat_axis=1, tiled=True)
    arrived = arrived.reshape(4, brick_size, seed_size * capacity, 128)
    summed_raw = lax.psum_scatter(arrived, "seed", scatter_dimension=2, tiled=True)
    own_rows = summed_raw[:, own_home, own_rank, :]
    mass_row = own_rows[0]
    moment_rows = own_rows[1:4] - mass_row[None] * own_seeds[0:3]
    result = jnp.concatenate([mass_row[None], moment_rows], axis=0)
    return result.reshape(4, lane_count * 128)


def solution(mesh):
    placed = (P(None, ("brick", "seed")), P(), P("brick", "seed"), P("brick"), P("brick", None))
    return jax.shard_map(
        body, mesh=mesh, in_specs=placed, out_specs=P(None, ("brick", "seed")), check_vma=False
    )
```

profile of v0, /device:TPU:0, one launch (start us, length us, event | category | flops | bytes accessed | tf_op | source)
XLA Modules:
  0.0 127.0 jit_solution(10801698994256494854)
XLA Ops:
  7.2 2.4 %scatter_custom_fusion.1 = s32[512]{0:T(512)S(1)} fusion(s32[512]{0:T(512)S(1)} %compare_select_fusion.7, s32[512]{0:T(512)S(1)} %iota.132, s32[]{:T(128)} %constant.488.clone.1), kind=kCustom, calls=%fused_computation.207 | custom fusion | bytes 2052 | tf_op jit(solution)/shard_map/scatter | solution.py:67
  10.8 2.2 %scatter_fusion.1 = f32[4,16,128]{2,0,1:T(4,128)} fusion(f32[4,16,128]{2,0,1:T(4,128)} %broadcast.1155.clone, s32[16]{0:T(128)S(1)} %get-tuple-element.468, f32[16,4,128]{2,1,0:T(4,128)S(1)} %bitcast.70), kind=kCustom, calls=%fused_computation.9 | custom fusion | bytes 98368 | tf_op jit(solution)/shard_map/scatter | solution.py:79
  13.0 8.3 %all-to-all-start = ((f32[4,16,128]{2,0,1:T(4,128)}), f32[4,16,128]{2,0,1:T(4,128)S(1)}, u32[]{:S(2)}, u32[]{:S(2)}) async-start(f32[4,16,128]{2,0,1:T(4,128)} %scatter_fusion.1), calls=%async_computation | async-start | bytes 65536 | tf_op jit(solution)/shard_map/all_to_all | solution.py:80
  22.7 0.8 gather_fusion.3
  23.8 4.9 %all-to-all-done = f32[4,16,128]{2,0,1:T(4,128)S(1)} async-done(((f32[4,16,128]{2,0,1:T(4,128)}), f32[4,16,128]{2,0,1:T(4,128)S(1)}, u32[]{:S(2)}, u32[]{:S(2)}) %all-to-all-start) | async-done | bytes 32800 | tf_op jit(solution)/shard_map/all_to_all | solution.py:80
  29.3 1.5 %scatter_fusion.2 = f32[4,16,128]{2,0,1:T(4,128)S(1)} fusion(f32[4,16,128]{2,0,1:T(4,128)S(1)} %broadcast.1155, s32[32]{0:T(128)S(1)} %get-tuple-element.469, f32[32,4,128]{2,1,0:T(4,128)S(1)} %gather_fusion.4), kind=kCustom, calls=%fused_computation.10 | custom fusion | bytes 196736 | tf_op jit(solution)/shard_map/scatter | solution.py:93
  30.9 1.9 %all_gather.15 = f32[4,32,128]{2,0,1:T(4,128)S(1)} all-gather(f32[4,16,128]{2,0,1:T(4,128)S(1)} %scatter_fusion.2), channel_id=1, replica_groups=mesh['brick'=16,'seed'=2] {'seed'}, dimensions={1}, use_global_device_ids=true | all-gather | bytes 98304 | tf_op jit(solution)/shard_map/all_gather | solution.py:94
  32.7 34.8 %while.35 = (s32[]{:T(128)}, f32[2,8,512]{2,1,0:T(8,128)S(1)}, f32[2,8,512]{2,1,0:T(8,128)S(1)}, s32[2]{0:T(128)S(1)}, pred[16,512]{1,0:T(8,128)(4,1)S(1)}, /*in...) while((s32[]{:T(128)}, f32[2,8,512]{2,1,0:T(8,128)S(1)}, ...), condition=%wide.region_8.9_spmd.clone, body=%wide.region_5.8_spmd.clone.sunk | while | flops 54553152 | bytes 820639 | solution.py:120
  35.2 4.3 %fusion.113 = f32[8,512]{1,0:T(8,128)S(1)} fusion(f32[8,512]{1,0:T(8,128)S(1)} %sub.605, f32[8,512]{1,0:T(8,128)S(1)} %broadcast_add_fusion.9, f32[8,512]{1,0:T(8,128)S(1)} %sub.606, f32[8,512]{1,0:T(8,128)S(1)} %broadcast_add_fusion.10, f32[8,512]{1,0:T(8,128)S(1)} %sub.607, f32[8,512]{1,0:T(8,128)S(1)} %broadcast_add_fusion.11, ...), kind=kLoop, calls=%fused_computation.16.clone.1 | loop fusion | flops 25161728 | bytes 135168 | tf_op jit(solution)/shard_map/while/body/eval_jaxpr/reduce_max | solution.py:115
  39.6 10.5 %select_reduce_fusion.2 = f32[8,512]{1,0:T(8,128)S(1)} fusion(f32[8,512]{1,0:T(8,128)S(1)} %fusion.113, f32[8,512]{1,0:T(8,128)S(1)} %sub.605, f32[8,512]{1,0:T(8,128)S(1)} %broadcast_add_fusion.9, f32[8,512]{1,0:T(8,128)S(1)} %sub.606, f32[8,512]{1,0:T(8,128)S(1)} %broadcast_add_fusion.10, f32[8,512]{1,0:T(8,128)S(1)} %sub.607, ...), kind=kLoop, calls=%fused_computation.14.clone.1 | loop fusion | flops 29356032 | bytes 151552 | tf_op jit(solution)/shard_map/while/body/eval_jaxpr/reduce_sum | solution.py:117
  52.6 4.3 %fusion.113 = f32[8,512]{1,0:T(8,128)S(1)} fusion(f32[8,512]{1,0:T(8,128)S(1)} %sub.605, f32[8,512]{1,0:T(8,128)S(1)} %broadcast_add_fusion.9, f32[8,512]{1,0:T(8,128)S(1)} %sub.606, f32[8,512]{1,0:T(8,128)S(1)} %broadcast_add_fusion.10, f32[8,512]{1,0:T(8,128)S(1)} %sub.607, f32[8,512]{1,0:T(8,128)S(1)} %broadcast_add_fusion.11, ...), kind=kLoop, calls=%fused_computation.16.clone.1 | loop fusion | flops 25161728 | bytes 135168 | tf_op jit(solution)/shard_map/while/body/eval_jaxpr/reduce_max | solution.py:115
  57.0 10.5 %select_reduce_fusion.2 = f32[8,512]{1,0:T(8,128)S(1)} fusion(f32[8,512]{1,0:T(8,128)S(1)} %fusion.113, f32[8,512]{1,0:T(8,128)S(1)} %sub.605, f32[8,512]{1,0:T(8,128)S(1)} %broadcast_add_fusion.9, f32[8,512]{1,0:T(8,128)S(1)} %sub.606, f32[8,512]{1,0:T(8,128)S(1)} %broadcast_add_fusion.10, f32[8,512]{1,0:T(8,128)S(1)} %sub.607, ...), kind=kLoop, calls=%fused_computation.14.clone.1 | loop fusion | flops 29356032 | bytes 151552 | tf_op jit(solution)/shard_map/while/body/eval_jaxpr/reduce_sum | solution.py:117
  67.5 1.9 %all-gather = f32[4,8,512]{2,1,0:T(8,128)S(1)} all-gather(f32[2,8,512]{2,1,0:T(8,128)S(1)} %get-tuple-element.337), channel_id=2, replica_groups=mesh['brick'=16,'seed'=2] {'seed'}, dimensions={0}, use_global_device_ids=true | all-gather | bytes 98304 | tf_op jit(solution)/shard_map/all_gather | solution.py:14
  69.3 1.8 %all-gather.1 = f32[4,8,512]{2,1,0:T(8,128)S(1)} all-gather(f32[2,8,512]{2,1,0:T(8,128)S(1)} %get-tuple-element.338), channel_id=3, replica_groups=mesh['brick'=16,'seed'=2] {'seed'}, dimensions={0}, use_global_device_ids=true | all-gather | bytes 98304 | tf_op jit(solution)/shard_map/all_gather | solution.py:14
  71.2 0.7 copy-done
  72.0 29.0 %while.36 = (s32[]{:T(128)}, f32[4,32,128]{2,0,1:T(4,128)S(1)}, s32[2]{0:T(128)S(1)}, s32[16,4]{1,0:T(8,128)S(1)}, pred[16,512]{1,0:T(8,128)(4,1)S(1)}, /*index=...) while((s32[]{:T(128)}, f32[4,32,128]{2,0,1:T(4,128)S(1)}, ...), condition=%wide.region_11.12_spmd.clone, body=%wide.region_9.11_spmd.clone.sunk | while | flops 130135552 | bytes 1242671 | solution.py:143
  74.5 10.3 %fusion.120 = f32[8,512,4]{1,2,0:T(4,128)S(1)} fusion(f32[8,512]{1,0:T(8,128)S(1)} %get-tuple-element.609, f32[8,512]{1,0:T(8,128)S(1)} %get-tuple-element.610, f32[8,512]{1,0:T(8,128)S(1)} %sub.625, f32[8,512]{1,0:T(8,128)S(1)} %get-tuple-element.617, f32[8,512]{1,0:T(8,128)S(1)} %sub.626, f32[8,512]{1,0:T(8,128)S(1)} %get-tuple-element.619, ...), kind=kOutput, calls=%fused_computation.78.clone.1 | convolution fusion | flops 130072576 | bytes 282624 | tf_op jit(solution)/shard_map/while/body/eval_jaxpr/fgi,gic->fgc/dot_general | solution.py:137
  84.8 1.7 %scatter_fusion = f32[4,32,128]{2,0,1:T(4,128)S(1)} fusion(f32[4,32,128]{2,0,1:T(4,128)S(1)} %get-tuple-element.681, s32[32]{0:T(128)S(1)} %fusion.115, f32[32,4,128]{2,1,0:T(4,128)S(1)} %bitcast.65), kind=kCustom, calls=%fused_computation.7.clone.clone.1 | custom fusion | flops 16384 | bytes 196736 | tf_op jit(solution)/shard_map/while/body/eval_jaxpr/scatter-add | solution.py:138
  89.0 10.3 %fusion.120 = f32[8,512,4]{1,2,0:T(4,128)S(1)} fusion(f32[8,512]{1,0:T(8,128)S(1)} %get-tuple-element.609, f32[8,512]{1,0:T(8,128)S(1)} %get-tuple-element.610, f32[8,512]{1,0:T(8,128)S(1)} %sub.625, f32[8,512]{1,0:T(8,128)S(1)} %get-tuple-element.617, f32[8,512]{1,0:T(8,128)S(1)} %sub.626, f32[8,512]{1,0:T(8,128)S(1)} %get-tuple-element.619, ...), kind=kOutput, calls=%fused_computation.78.clone.1 | convolution fusion | flops 130072576 | bytes 282624 | tf_op jit(solution)/shard_map/while/body/eval_jaxpr/fgi,gic->fgc/dot_general | solution.py:137
  99.3 1.7 %scatter_fusion = f32[4,32,128]{2,0,1:T(4,128)S(1)} fusion(f32[4,32,128]{2,0,1:T(4,128)S(1)} %get-tuple-element.681, s32[32]{0:T(128)S(1)} %fusion.115, f32[32,4,128]{2,1,0:T(4,128)S(1)} %bitcast.65), kind=kCustom, calls=%fused_computation.7.clone.clone.1 | custom fusion | flops 16384 | bytes 196736 | tf_op jit(solution)/shard_map/while/body/eval_jaxpr/scatter-add | solution.py:138
  101.6 1.5 %scatter_fusion.3 = f32[4,32,128]{2,0,1:T(4,128)S(1)} fusion(f32[4,32,128]{2,0,1:T(4,128)S(1)} %broadcast.1150, s32[32]{0:T(128)S(1)} %get-tuple-element.452, f32[32,4,128]{2,1,0:T(4,128)S(1)} %gather_fusion.5), kind=kCustom, calls=%fused_computation.11 | custom fusion | bytes 196736 | tf_op jit(solution)/shard_map/scatter | solution.py:146
  103.1 10.1 %all_to_all.10 = f32[4,32,128]{2,0,1:T(4,128)S(1)} all-to-all(f32[4,32,128]{2,0,1:T(4,128)S(1)} %scatter_fusion.3), channel_id=1, replica_groups=mesh['brick'=16,'seed'=2] {'brick'}, dimensions={1} | all-to-all | bytes 131072 | tf_op jit(solution)/shard_map/all_to_all | solution.py:147
  113.8 4.3 %reduce-scatter.2.cloned.1.call-done = f32[4,16,1,128]{3,1,0,2:T(8,128)} async-done(((f32[4,16,2,128]{3,1,0,2:T(8,128)}), f32[4,16,1,128]{3,1,0,2:T(8,128)}) %reduce-scatter.2.cloned.1.call-update) | async-done | bytes 32784 | tf_op jit(solution)/shard_map/reduce_scatter | solution.py:149
  118.1 0.8 copy.39
  (145 shorter events, 13.7 us)
Async XLA Ops:
  9.8 1.0 copy-start.1
  10.8 10.6 %copy-start.2 = (s32[512]{0:T(512)S(1)}, s32[512]{0:T(512)}, u32[]{:S(2)}) copy-start(s32[512]{0:T(512)} %param.10) | copy-start | bytes 6148
  13.0 15.7 %all-to-all-start = ((f32[4,16,128]{2,0,1:T(4,128)}), f32[4,16,128]{2,0,1:T(4,128)S(1)}, u32[]{:S(2)}, u32[]{:S(2)}) async-start(f32[4,16,128]{2,0,1:T(4,128)} %scatter_fusion.1), calls=%async_computation | async-start | bytes 65536 | tf_op jit(solution)/shard_map/all_to_all | solution.py:80
  21.3 96.8 %reduce-scatter.2.cloned.1.call-start = ((), (), s32[]{:S(2)}) async-start(), calls=%async_computation.3 | async-start | bytes 98304 | tf_op jit(solution)/shard_map/reduce_scatter | solution.py:149
  21.5 1.0 copy-start.3
  22.7 0.9 copy-start.4
  71.2 0.8 copy-start
Sparse Core Ops, SparseCore 0:
  114.0 4.1 reduce-scatter.1
where the time goes:
time: 127 us
  other arithmetic  36 us (28%)
  local copies, waits for them, and re-layouts  20.5 us (16%)
  matrix products  20.5 us (16%)
  blocking collectives  15.7 us (12%)
  between operations  13.6 us (11%)
  waiting for transfers between devices  9.24 us (7%)
  starting transfers between devices  8.35 us (7%)
  loops' own time  3.11 us (2%)
    reduce_sum x2, other arithmetic, local_both(): return (pixel_peak, jnp.sum(raw_share, axis=2))  21 us
    dot_general x2, matrix products, contribute(): jnp.einsum('fgi,gic->fgc', features, shares, precision=lax.Precision.HIGH...  20.5 us
    all_to_all x1, blocking collectives, body(): lax.all_to_all(outgoing_raw, 'brick', split_axis=1, concat_axis=1, tiled=...  10.1 us
    reduce_max x2, other arithmetic, local_both(): pixel_peak = jnp.max(scores, axis=2)  8.68 us
    all_to_all x1, starting transfers between devices, body(): lax.all_to_all(outgoing, 'brick', split_axis=1, concat_axis=1, tiled=True)  8.31 us
    all_to_all x1, waiting for transfers between devices, body(): lax.all_to_all(outgoing, 'brick', split_axis=1, concat_axis=1, tiled=True)  4.92 us
    reduce_scatter x1, waiting for transfers between devices, body(): lax.psum_scatter(arrived, 'seed', scatter_dimension=2, tiled=True)  4.3 us
    all_gather x2, blocking collectives, joined(): pieces = jax.tree.map(lambda part: lax.all_gather(part, axis), value)  3.69 us
  transfers between devices with their start and end apart: 2, of which 2 were waited for; matrix products, arithmetic and copies ran while one was open for 2% of the time, Pallas kernels for 0%

commit v1 on v0

--- a/solution.py
+++ b/solution.py
@@ -144,7 +144,15 @@
     raw_target = home_owner * (seed_size * capacity) + home_shard * capacity + home_rank
     outgoing_raw = jnp.zeros((4, brick_size * seed_size * capacity, 128), jnp.float32)
     outgoing_raw = outgoing_raw.at[:, raw_target, :].set(totals[:, panel_index, :])
-    arrived = lax.all_to_all(outgoing_raw, "brick", split_axis=1, concat_axis=1, tiled=True)
+    ways, here = (lax.axis_size("brick"), lax.axis_index("brick"))
+    width = outgoing_raw.shape[1] // ways
+    turned = jnp.roll(outgoing_raw, -here * width, axis=1)
+    got = [lax.slice_in_dim(turned, 0, width, axis=1)]
+    for far in range(1, ways):
+        sent = lax.slice_in_dim(turned, far * width, (far + 1) * width, axis=1)
+        got.append(lax.ppermute(sent, "brick", [(d, (d + far) % ways) for d in range(ways)]))
+    line = jnp.concatenate(got[::-1], axis=1)
+    arrived = jnp.roll(line, (here + 1) * got[0].shape[1], axis=1)
     arrived = arrived.reshape(4, brick_size, seed_size * capacity, 128)
     summed_raw = lax.psum_scatter(arrived, "seed", scatter_dimension=2, tiled=True)
     own_rows = summed_raw[:, own_home, own_rank, :]

time: 127 us -> 148 us (1.17)
  starting transfers between devices: 8.35 us -> 31.8 us
  blocking collectives: 15.7 us -> 5.55 us
  waiting for transfers between devices: 9.24 us -> 16 us
    ppermute x0 -> x15, starting transfers between devices: none -> 23.3 us  [body(): lax.ppermute(sent, 'brick', [(d, (d + far) % ways) for d in range(ways)])]
    all_to_all x1 -> x0, blocking collectives: 10.1 us -> none  [body(): lax.all_to_all(outgoing_raw, 'brick', split_axis=1, concat_axis=1, tiled=...]
    ppermute x0 -> x15, waiting for transfers between devices: none -> 7.16 us  [body(): lax.ppermute(sent, 'brick', [(d, (d + far) % ways) for d in range(ways)])]
  transfers between devices with their start and end apart: 2 -> 17, of which waited for: 2 -> 5; matrix products, arithmetic and copies ran while one was open for 2% -> 2% of each run, Pallas kernels for 0% -> 0%
where the time goes in v1:
time: 148 us
  other arithmetic  36.2 us (24%)
  starting transfers between devices  31.8 us (21%)
  local copies, waits for them, and re-layouts  20.6 us (14%)
  matrix products  20.5 us (14%)
  waiting for transfers between devices  16 us (11%)
  between operations  13.7 us (9%)
  blocking collectives  5.55 us (4%)
  loops' own time  3.11 us (2%)
    ppermute x15, starting transfers between devices, body(): lax.ppermute(sent, 'brick', [(d, (d + far) % ways) for d in range(ways)])  23.3 us
    reduce_sum x2, other arithmetic, local_both(): return (pixel_peak, jnp.sum(raw_share, axis=2))  21 us
    dot_general x2, matrix products, contribute(): jnp.einsum('fgi,gic->fgc', features, shares, precision=lax.Precision.HIGH...  20.5 us
    reduce_max x2, other arithmetic, local_both(): pixel_peak = jnp.max(scores, axis=2)  8.68 us
    all_to_all x1, starting transfers between devices, body(): lax.all_to_all(outgoing, 'brick', split_axis=1, concat_axis=1, tiled=True)  8.44 us
    ppermute x15, waiting for transfers between devices, body(): lax.ppermute(sent, 'brick', [(d, (d + far) % ways) for d in range(ways)])  7.16 us
    all_to_all x1, waiting for transfers between devices, body(): lax.all_to_all(outgoing, 'brick', split_axis=1, concat_axis=1, tiled=True)  4.89 us
    reduce_scatter x1, waiting for transfers between devices, body(): lax.psum_scatter(arrived, 'seed', scatter_dimension=2, tiled=True)  3.91 us
  transfers between devices with their start and end apart: 17, of which 5 were waited for; matrix products, arithmetic and copies ran while one was open for 2% of the time, Pallas kernels for 0%

profile of v1, /device:TPU:0, one launch (start us, length us, event | category | flops | bytes accessed | tf_op | source)
XLA Modules:
  0.0 147.5 jit_solution(6353142195067069562)
XLA Ops:
  7.2 2.4 %scatter_custom_fusion.1 = s32[512]{0:T(512)S(1)} fusion(s32[512]{0:T(512)S(1)} %compare_select_fusion.7, s32[512]{0:T(512)S(1)} %iota.132, s32[]{:T(128)} %constant.506.clone.1), kind=kCustom, calls=%fused_computation.229 | custom fusion | bytes 2052 | tf_op jit(solution)/shard_map/scatter | solution.py:67
  10.8 2.2 %scatter_fusion.1 = f32[4,16,128]{2,0,1:T(4,128)} fusion(f32[4,16,128]{2,0,1:T(4,128)} %broadcast.1156.clone, s32[16]{0:T(128)S(1)} %get-tuple-element.484, f32[16,4,128]{2,1,0:T(4,128)S(1)} %bitcast.70), kind=kCustom, calls=%fused_computation.9 | custom fusion | bytes 98368 | tf_op jit(solution)/shard_map/scatter | solution.py:79
  13.0 8.4 %all-to-all-start = ((f32[4,16,128]{2,0,1:T(4,128)}), f32[4,16,128]{2,0,1:T(4,128)S(1)}, u32[]{:S(2)}, u32[]{:S(2)}) async-start(f32[4,16,128]{2,0,1:T(4,128)} %scatter_fusion.1), calls=%async_computation | async-start | bytes 65536 | tf_op jit(solution)/shard_map/all_to_all | solution.py:80
  23.9 4.9 %all-to-all-done = f32[4,16,128]{2,0,1:T(4,128)S(1)} async-done(((f32[4,16,128]{2,0,1:T(4,128)}), f32[4,16,128]{2,0,1:T(4,128)S(1)}, u32[]{:S(2)}, u32[]{:S(2)}) %all-to-all-start) | async-done | bytes 32800 | tf_op jit(solution)/shard_map/all_to_all | solution.py:80
  31.0 1.9 %all_gather.15 = f32[4,32,128]{2,0,1:T(4,128)S(1)} all-gather(f32[4,16,128]{2,0,1:T(4,128)S(1)} %scatter_fusion.2), channel_id=1, replica_groups=mesh['brick'=16,'seed'=2] {'seed'}, dimensions={1}, use_global_device_ids=true | all-gather | bytes 98304 | tf_op jit(solution)/shard_map/all_gather | solution.py:94
  32.9 34.8 %while.35 = (s32[]{:T(128)}, f32[2,8,512]{2,1,0:T(8,128)S(1)}, f32[2,8,512]{2,1,0:T(8,128)S(1)}, s32[2]{0:T(128)S(1)}, pred[16,512]{1,0:T(8,128)(4,1)S(1)}, /*in...) while((s32[]{:T(128)}, f32[2,8,512]{2,1,0:T(8,128)S(1)}, ...), condition=%wide.region_8.9_spmd.clone, body=%wide.region_5.8_spmd.clone.sunk | while | flops 54553152 | bytes 820639 | solution.py:120
  35.4 4.3 %fusion.116 = f32[8,512]{1,0:T(8,128)S(1)} fusion(f32[8,512]{1,0:T(8,128)S(1)} %sub.611, f32[8,512]{1,0:T(8,128)S(1)} %broadcast_add_fusion.9, f32[8,512]{1,0:T(8,128)S(1)} %sub.612, f32[8,512]{1,0:T(8,128)S(1)} %broadcast_add_fusion.10, f32[8,512]{1,0:T(8,128)S(1)} %sub.613, f32[8,512]{1,0:T(8,128)S(1)} %broadcast_add_fusion.11, ...), kind=kLoop, calls=%fused_computation.16.clone.1 | loop fusion | flops 25161728 | bytes 135168 | tf_op jit(solution)/shard_map/while/body/eval_jaxpr/reduce_max | solution.py:115
  39.7 10.5 %select_reduce_fusion.2 = f32[8,512]{1,0:T(8,128)S(1)} fusion(f32[8,512]{1,0:T(8,128)S(1)} %fusion.116, f32[8,512]{1,0:T(8,128)S(1)} %sub.611, f32[8,512]{1,0:T(8,128)S(1)} %broadcast_add_fusion.9, f32[8,512]{1,0:T(8,128)S(1)} %sub.612, f32[8,512]{1,0:T(8,128)S(1)} %broadcast_add_fusion.10, f32[8,512]{1,0:T(8,128)S(1)} %sub.613, ...), kind=kLoop, calls=%fused_computation.14.clone.1 | loop fusion | flops 29356032 | bytes 151552 | tf_op jit(solution)/shard_map/while/body/eval_jaxpr/reduce_sum | solution.py:117
  52.8 4.3 %fusion.116 = f32[8,512]{1,0:T(8,128)S(1)} fusion(f32[8,512]{1,0:T(8,128)S(1)} %sub.611, f32[8,512]{1,0:T(8,128)S(1)} %broadcast_add_fusion.9, f32[8,512]{1,0:T(8,128)S(1)} %sub.612, f32[8,512]{1,0:T(8,128)S(1)} %broadcast_add_fusion.10, f32[8,512]{1,0:T(8,128)S(1)} %sub.613, f32[8,512]{1,0:T(8,128)S(1)} %broadcast_add_fusion.11, ...), kind=kLoop, calls=%fused_computation.16.clone.1 | loop fusion | flops 25161728 | bytes 135168 | tf_op jit(solution)/shard_map/while/body/eval_jaxpr/reduce_max | solution.py:115
  57.1 10.5 %select_reduce_fusion.2 = f32[8,512]{1,0:T(8,128)S(1)} fusion(f32[8,512]{1,0:T(8,128)S(1)} %fusion.116, f32[8,512]{1,0:T(8,128)S(1)} %sub.611, f32[8,512]{1,0:T(8,128)S(1)} %broadcast_add_fusion.9, f32[8,512]{1,0:T(8,128)S(1)} %sub.612, f32[8,512]{1,0:T(8,128)S(1)} %broadcast_add_fusion.10, f32[8,512]{1,0:T(8,128)S(1)} %sub.613, ...), kind=kLoop, calls=%fused_computation.14.clone.1 | loop fusion | flops 29356032 | bytes 151552 | tf_op jit(solution)/shard_map/while/body/eval_jaxpr/reduce_sum | solution.py:117
  67.6 1.9 %all-gather = f32[4,8,512]{2,1,0:T(8,128)S(1)} all-gather(f32[2,8,512]{2,1,0:T(8,128)S(1)} %get-tuple-element.338), channel_id=2, replica_groups=mesh['brick'=16,'seed'=2] {'seed'}, dimensions={0}, use_global_device_ids=true | all-gather | bytes 98304 | tf_op jit(solution)/shard_map/all_gather | solution.py:14
  69.5 1.8 %all-gather.1 = f32[4,8,512]{2,1,0:T(8,128)S(1)} all-gather(f32[2,8,512]{2,1,0:T(8,128)S(1)} %get-tuple-element.339), channel_id=3, replica_groups=mesh['brick'=16,'seed'=2] {'seed'}, dimensions={0}, use_global_device_ids=true | all-gather | bytes 98304 | tf_op jit(solution)/shard_map/all_gather | solution.py:14
  72.1 29.0 %while.36 = (s32[]{:T(128)}, f32[4,32,128]{2,0,1:T(4,128)S(1)}, s32[2]{0:T(128)S(1)}, s32[16,4]{1,0:T(8,128)S(1)}, pred[16,512]{1,0:T(8,128)(4,1)S(1)}, /*index=...) while((s32[]{:T(128)}, f32[4,32,128]{2,0,1:T(4,128)S(1)}, ...), condition=%wide.region_11.12_spmd.clone, body=%wide.region_9.11_spmd.clone.sunk | while | flops 130135552 | bytes 1242671 | solution.py:143
  74.7 10.3 %fusion.123 = f32[8,512,4]{1,2,0:T(4,128)S(1)} fusion(f32[8,512]{1,0:T(8,128)S(1)} %get-tuple-element.625, f32[8,512]{1,0:T(8,128)S(1)} %get-tuple-element.626, f32[8,512]{1,0:T(8,128)S(1)} %sub.631, f32[8,512]{1,0:T(8,128)S(1)} %get-tuple-element.633, f32[8,512]{1,0:T(8,128)S(1)} %sub.632, f32[8,512]{1,0:T(8,128)S(1)} %get-tuple-element.635, ...), kind=kOutput, calls=%fused_computation.78.clone.1 | convolution fusion | flops 130072576 | bytes 282624 | tf_op jit(solution)/shard_map/while/body/eval_jaxpr/fgi,gic->fgc/dot_general | solution.py:137
  84.9 1.7 %scatter_fusion = f32[4,32,128]{2,0,1:T(4,128)S(1)} fusion(f32[4,32,128]{2,0,1:T(4,128)S(1)} %get-tuple-element.697, s32[32]{0:T(128)S(1)} %fusion.118, f32[32,4,128]{2,1,0:T(4,128)S(1)} %bitcast.65), kind=kCustom, calls=%fused_computation.7.clone.clone.1 | custom fusion | flops 16384 | bytes 196736 | tf_op jit(solution)/shard_map/while/body/eval_jaxpr/scatter-add | solution.py:138
  89.1 10.3 %fusion.123 = f32[8,512,4]{1,2,0:T(4,128)S(1)} fusion(f32[8,512]{1,0:T(8,128)S(1)} %get-tuple-element.625, f32[8,512]{1,0:T(8,128)S(1)} %get-tuple-element.626, f32[8,512]{1,0:T(8,128)S(1)} %sub.631, f32[8,512]{1,0:T(8,128)S(1)} %get-tuple-element.633, f32[8,512]{1,0:T(8,128)S(1)} %sub.632, f32[8,512]{1,0:T(8,128)S(1)} %get-tuple-element.635, ...), kind=kOutput, calls=%fused_computation.78.clone.1 | convolution fusion | flops 130072576 | bytes 282624 | tf_op jit(solution)/shard_map/while/body/eval_jaxpr/fgi,gic->fgc/dot_general | solution.py:137
  99.4 1.7 %scatter_fusion = f32[4,32,128]{2,0,1:T(4,128)S(1)} fusion(f32[4,32,128]{2,0,1:T(4,128)S(1)} %get-tuple-element.697, s32[32]{0:T(128)S(1)} %fusion.118, f32[32,4,128]{2,1,0:T(4,128)S(1)} %bitcast.65), kind=kCustom, calls=%fused_computation.7.clone.clone.1 | custom fusion | flops 16384 | bytes 196736 | tf_op jit(solution)/shard_map/while/body/eval_jaxpr/scatter-add | solution.py:138
  108.4 2.4 %collective-permute-start.4 = (f32[4,2,128]{2,0,1:T(4,128)S(1)}, f32[4,2,128]{2,0,1:T(4,128)S(1)}, u32[]{:S(2)}, u32[]{:S(2)}) collective-permute-start(f32[4,2,128]{2,0,1:T(4,128)S(1)} %get-tuple-element.478), channel_id=1, source_target_pairs={{0,22},{2,24},{4,26},{6,28},{8,30},{10,0},{12,2},{14,4},{16,6},{18... | collective-permute-start | bytes 12296 | tf_op jit(solution)/shard_map/ppermute | solution.py:153
  114.7 3.7 %collective-permute-start.8 = (f32[4,2,128]{2,0,1:T(4,128)S(1)}, f32[4,2,128]{2,0,1:T(4,128)S(1)}, u32[]{:S(2)}, u32[]{:S(2)}) collective-permute-start(f32[4,2,128]{2,0,1:T(4,128)S(1)} %get-tuple-element.474), channel_id=1, source_target_pairs={{0,14},{2,16},{4,18},{6,20},{8,22},{10,24},{12,26},{14,28},{16,30}... | collective-permute-start | bytes 12296 | tf_op jit(solution)/shard_map/ppermute | solution.py:153
  120.0 1.6 %collective-permute-start.11 = (f32[4,2,128]{2,0,1:T(4,128)S(1)}, f32[4,2,128]{2,0,1:T(4,128)S(1)}, u32[]{:S(2)}, u32[]{:S(2)}) collective-permute-start(f32[4,2,128]{2,0,1:T(4,128)S(1)} %get-tuple-element.471), channel_id=1, source_target_pairs={{0,8},{2,10},{4,12},{6,14},{8,16},{10,18},{12,20},{14,22},{16,24},... | collective-permute-start | bytes 12296 | tf_op jit(solution)/shard_map/ppermute | solution.py:153
  121.6 3.6 %collective-permute-start.12 = (f32[4,2,128]{2,0,1:T(4,128)S(1)}, f32[4,2,128]{2,0,1:T(4,128)S(1)}, u32[]{:S(2)}, u32[]{:S(2)}) collective-permute-start(f32[4,2,128]{2,0,1:T(4,128)S(1)} %get-tuple-element.470), channel_id=1, source_target_pairs={{0,6},{2,8},{4,10},{6,12},{8,14},{10,16},{12,18},{14,20},{16,22},{... | collective-permute-start | bytes 12296 | tf_op jit(solution)/shard_map/ppermute | solution.py:153
  128.2 3.4 %collective-permute-done.13 = f32[4,2,128]{2,0,1:T(4,128)S(1)} collective-permute-done((f32[4,2,128]{2,0,1:T(4,128)S(1)}, f32[4,2,128]{2,0,1:T(4,128)S(1)}, u32[]{:S(2)}, u32[]{:S(2)}) %collective-permute-start.13) | collective-permute-done | bytes 4128 | tf_op jit(solution)/shard_map/ppermute | solution.py:153
  131.6 2.4 %collective-permute-done.14 = f32[4,2,128]{2,0,1:T(4,128)S(1)} collective-permute-done((f32[4,2,128]{2,0,1:T(4,128)S(1)}, f32[4,2,128]{2,0,1:T(4,128)S(1)}, u32[]{:S(2)}, u32[]{:S(2)}) %collective-permute-start.14) | collective-permute-done | bytes 4128 | tf_op jit(solution)/shard_map/ppermute | solution.py:153
  134.7 3.9 %reduce-scatter.2.cloned.1.call-done = f32[4,16,1,128]{3,1,0,2:T(8,128)} async-done(((f32[4,16,2,128]{3,1,0,2:T(8,128)}), f32[4,16,1,128]{3,1,0,2:T(8,128)}) %reduce-scatter.2.cloned.1.call-update) | async-done | bytes 32784 | tf_op jit(solution)/shard_map/reduce_scatter | solution.py:157
  (193 shorter events, 32.7 us)
Async XLA Ops:
  9.8 1.0 copy-start.1
  13.0 8.5 %copy-start.2 = (s32[512]{0:T(512)S(1)}, s32[512]{0:T(512)}, u32[]{:S(2)}) copy-start(s32[512]{0:T(512)} %param.12) | copy-start | bytes 6148
  13.0 15.9 %all-to-all-start = ((f32[4,16,128]{2,0,1:T(4,128)}), f32[4,16,128]{2,0,1:T(4,128)S(1)}, u32[]{:S(2)}, u32[]{:S(2)}) async-start(f32[4,16,128]{2,0,1:T(4,128)} %scatter_fusion.1), calls=%async_computation | async-start | bytes 65536 | tf_op jit(solution)/shard_map/all_to_all | solution.py:80
  21.4 117.2 %reduce-scatter.2.cloned.1.call-start = ((), (), s32[]{:S(2)}) async-start(), calls=%async_computation.2 | async-start | bytes 98304 | tf_op jit(solution)/shard_map/reduce_scatter | solution.py:157
  21.6 1.0 copy-start.3
  22.8 0.9 copy-start.4
  71.4 0.8 copy-start
  103.3 7.5 %collective-permute-start = (f32[4,2,128]{2,0,1:T(4,128)S(1)}, f32[4,2,128]{2,0,1:T(4,128)S(1)}, u32[]{:S(2)}, u32[]{:S(2)}) collective-permute-start(f32[4,2,128]{2,0,1:T(4,128)S(1)} %get-tuple-element.482), channel_id=1, source_target_pairs={{0,30},{2,0},{4,2},{6,4},{8,6},{10,8},{12,10},{14,12},{16,14},{18,... | collective-permute-start | bytes 12296 | tf_op jit(solution)/shard_map/ppermute | solution.py:153
  104.2 8.1 %collective-permute-start.1 = (f32[4,2,128]{2,0,1:T(4,128)S(1)}, f32[4,2,128]{2,0,1:T(4,128)S(1)}, u32[]{:S(2)}, u32[]{:S(2)}) collective-permute-start(f32[4,2,128]{2,0,1:T(4,128)S(1)} %get-tuple-element.481), channel_id=1, source_target_pairs={{0,28},{2,30},{4,0},{6,2},{8,4},{10,6},{12,8},{14,10},{16,12},{18,... | collective-permute-start | bytes 12296 | tf_op jit(solution)/shard_map/ppermute | solution.py:153
  105.6 8.1 %collective-permute-start.2 = (f32[4,2,128]{2,0,1:T(4,128)S(1)}, f32[4,2,128]{2,0,1:T(4,128)S(1)}, u32[]{:S(2)}, u32[]{:S(2)}) collective-permute-start(f32[4,2,128]{2,0,1:T(4,128)S(1)} %get-tuple-element.480), channel_id=1, source_target_pairs={{0,26},{2,28},{4,30},{6,0},{8,2},{10,4},{12,6},{14,8},{16,10},{18,... | collective-permute-start | bytes 12296 | tf_op jit(solution)/shard_map/ppermute | solution.py:153
  107.0 7.7 %collective-permute-start.3 = (f32[4,2,128]{2,0,1:T(4,128)S(1)}, f32[4,2,128]{2,0,1:T(4,128)S(1)}, u32[]{:S(2)}, u32[]{:S(2)}) collective-permute-start(f32[4,2,128]{2,0,1:T(4,128)S(1)} %get-tuple-element.479), channel_id=1, source_target_pairs={{0,24},{2,26},{4,28},{6,30},{8,0},{10,2},{12,4},{14,6},{16,8},{18,... | collective-permute-start | bytes 12296 | tf_op jit(solution)/shard_map/ppermute | solution.py:153
  108.4 10.0 %collective-permute-start.4 = (f32[4,2,128]{2,0,1:T(4,128)S(1)}, f32[4,2,128]{2,0,1:T(4,128)S(1)}, u32[]{:S(2)}, u32[]{:S(2)}) collective-permute-start(f32[4,2,128]{2,0,1:T(4,128)S(1)} %get-tuple-element.478), channel_id=1, source_target_pairs={{0,22},{2,24},{4,26},{6,28},{8,30},{10,0},{12,2},{14,4},{16,6},{18... | collective-permute-start | bytes 12296 | tf_op jit(solution)/shard_map/ppermute | solution.py:153
  110.8 9.1 %collective-permute-start.5 = (f32[4,2,128]{2,0,1:T(4,128)S(1)}, f32[4,2,128]{2,0,1:T(4,128)S(1)}, u32[]{:S(2)}, u32[]{:S(2)}) collective-permute-start(f32[4,2,128]{2,0,1:T(4,128)S(1)} %get-tuple-element.477), channel_id=1, source_target_pairs={{0,20},{2,22},{4,24},{6,26},{8,28},{10,30},{12,0},{14,2},{16,4},{1... | collective-permute-start | bytes 12296 | tf_op jit(solution)/shard_map/ppermute | solution.py:153
  112.3 7.7 %collective-permute-start.6 = (f32[4,2,128]{2,0,1:T(4,128)S(1)}, f32[4,2,128]{2,0,1:T(4,128)S(1)}, u32[]{:S(2)}, u32[]{:S(2)}) collective-permute-start(f32[4,2,128]{2,0,1:T(4,128)S(1)} %get-tuple-element.476), channel_id=1, source_target_pairs={{0,18},{2,20},{4,22},{6,24},{8,26},{10,28},{12,30},{14,0},{16,2},{... | collective-permute-start | bytes 12296 | tf_op jit(solution)/shard_map/ppermute | solution.py:153
  113.7 7.9 %collective-permute-start.7 = (f32[4,2,128]{2,0,1:T(4,128)S(1)}, f32[4,2,128]{2,0,1:T(4,128)S(1)}, u32[]{:S(2)}, u32[]{:S(2)}) collective-permute-start(f32[4,2,128]{2,0,1:T(4,128)S(1)} %get-tuple-element.475), channel_id=1, source_target_pairs={{0,16},{2,18},{4,20},{6,22},{8,24},{10,26},{12,28},{14,30},{16,0},... | collective-permute-start | bytes 12296 | tf_op jit(solution)/shard_map/ppermute | solution.py:153
  114.7 10.6 %collective-permute-start.8 = (f32[4,2,128]{2,0,1:T(4,128)S(1)}, f32[4,2,128]{2,0,1:T(4,128)S(1)}, u32[]{:S(2)}, u32[]{:S(2)}) collective-permute-start(f32[4,2,128]{2,0,1:T(4,128)S(1)} %get-tuple-element.474), channel_id=1, source_target_pairs={{0,14},{2,16},{4,18},{6,20},{8,22},{10,24},{12,26},{14,28},{16,30}... | collective-permute-start | bytes 12296 | tf_op jit(solution)/shard_map/ppermute | solution.py:153
  118.4 8.3 %collective-permute-start.9 = (f32[4,2,128]{2,0,1:T(4,128)S(1)}, f32[4,2,128]{2,0,1:T(4,128)S(1)}, u32[]{:S(2)}, u32[]{:S(2)}) collective-permute-start(f32[4,2,128]{2,0,1:T(4,128)S(1)} %get-tuple-element.473), channel_id=1, source_target_pairs={{0,12},{2,14},{4,16},{6,18},{8,20},{10,22},{12,24},{14,26},{16,28}... | collective-permute-start | bytes 12296 | tf_op jit(solution)/shard_map/ppermute | solution.py:153
  120.0 6.8 %collective-permute-start.10 = (f32[4,2,128]{2,0,1:T(4,128)S(1)}, f32[4,2,128]{2,0,1:T(4,128)S(1)}, u32[]{:S(2)}, u32[]{:S(2)}) collective-permute-start(f32[4,2,128]{2,0,1:T(4,128)S(1)} %get-tuple-element.472), channel_id=1, source_target_pairs={{0,10},{2,12},{4,14},{6,16},{8,18},{10,20},{12,22},{14,24},{16,26}... | collective-permute-start | bytes 12296 | tf_op jit(solution)/shard_map/ppermute | solution.py:153
  120.0 6.8 %collective-permute-start.11 = (f32[4,2,128]{2,0,1:T(4,128)S(1)}, f32[4,2,128]{2,0,1:T(4,128)S(1)}, u32[]{:S(2)}, u32[]{:S(2)}) collective-permute-start(f32[4,2,128]{2,0,1:T(4,128)S(1)} %get-tuple-element.471), channel_id=1, source_target_pairs={{0,8},{2,10},{4,12},{6,14},{8,16},{10,18},{12,20},{14,22},{16,24},... | collective-permute-start | bytes 12296 | tf_op jit(solution)/shard_map/ppermute | solution.py:153
  121.6 6.6 %collective-permute-start.12 = (f32[4,2,128]{2,0,1:T(4,128)S(1)}, f32[4,2,128]{2,0,1:T(4,128)S(1)}, u32[]{:S(2)}, u32[]{:S(2)}) collective-permute-start(f32[4,2,128]{2,0,1:T(4,128)S(1)} %get-tuple-element.470), channel_id=1, source_target_pairs={{0,6},{2,8},{4,10},{6,12},{8,14},{10,16},{12,18},{14,20},{16,22},{... | collective-permute-start | bytes 12296 | tf_op jit(solution)/shard_map/ppermute | solution.py:153
  125.3 6.3 %collective-permute-start.13 = (f32[4,2,128]{2,0,1:T(4,128)S(1)}, f32[4,2,128]{2,0,1:T(4,128)S(1)}, u32[]{:S(2)}, u32[]{:S(2)}) collective-permute-start(f32[4,2,128]{2,0,1:T(4,128)S(1)} %get-tuple-element.469), channel_id=1, source_target_pairs={{0,4},{2,6},{4,8},{6,10},{8,12},{10,14},{12,16},{14,18},{16,20},{1... | collective-permute-start | bytes 12296 | tf_op jit(solution)/shard_map/ppermute | solution.py:153
  126.8 7.2 %collective-permute-start.14 = (f32[4,2,128]{2,0,1:T(4,128)S(1)}, f32[4,2,128]{2,0,1:T(4,128)S(1)}, u32[]{:S(2)}, u32[]{:S(2)}) collective-permute-start(f32[4,2,128]{2,0,1:T(4,128)S(1)} %get-tuple-element.468), channel_id=1, source_target_pairs={{0,2},{2,4},{4,6},{6,8},{8,10},{10,12},{12,14},{14,16},{16,18},{18... | collective-permute-start | bytes 12296 | tf_op jit(solution)/shard_map/ppermute | solution.py:153
Sparse Core Ops, SparseCore 0:
  134.9 3.7 reduce-scatter.1
